TPU v7x, 32 devices: a whole 2x2x4 slice. The times are simulated.
32 devices in a mesh: dp: 8 (over y, x, core), tensor: 4 (over z).
Axes of the slice: x: 2, y: 2, z: 4, core: 2. Of those that a mesh axis runs over, the one named last changes fastest.
Arguments:
- hidden_in: bfloat16 [3, 4096, 768], P(None, ('dp', 'tensor')), may hold values from -6 to 6
- segment_ids: int32 [3, 32, 128], P(None, ('dp', 'tensor')), may hold values from 0 to 7, never falling along the last dimension, each value on 1 to 32 neighbouring positions
- pooled_grad: float32 [3, 32, 8, 768], P(None, ('dp', 'tensor')), may hold values from -96 to 96
- qkv_weight: bfloat16 [3, 768, 768], P(None, 'dp', 'tensor'), may hold values from -0.21875 to 0.21875
- qv_bias: bfloat16 [2, 768], P(None, ('dp', 'tensor')), may hold values from -1.1953125 to 1.1953125
- out_weight: bfloat16 [768, 768], P('tensor', 'dp'), may hold values from -0.875 to 0.875
- out_bias: bfloat16 [768], P(('dp', 'tensor')), may hold values from -1.1953125 to 1.1953125
- norm1_gain: bfloat16 [768], P(('dp', 'tensor')), may hold values from 0.099609375 to 1.8984375
- norm1_shift: bfloat16 [768], P(('dp', 'tensor')), may hold values from -1.1953125 to 1.1953125
- up_weight: bfloat16 [768, 3072], P('dp', 'tensor'), may hold values from -0.21875 to 0.21875
- up_bias: bfloat16 [3072], P(('dp', 'tensor')), may hold values from -1.1953125 to 1.1953125
- down_weight: bfloat16 [3072, 768], P('tensor', 'dp'), may hold values from -0.109375 to 0.109375
- down_bias: bfloat16 [768], P(('dp', 'tensor')), may hold values from -1.1953125 to 1.1953125
- norm2_gain: bfloat16 [768], P(('dp', 'tensor')), may hold values from 0.099609375 to 1.8984375
- norm2_shift: bfloat16 [768], P(('dp', 'tensor')), may hold values from -1.1953125 to 1.1953125
Outputs:
- pooled_out: float32 [3, 32, 8, 768], P(None, ('dp', 'tensor'))
- input_grad: float32 [3, 4096, 768], P(None, ('dp', 'tensor'))
- qkv_weight_grad: float32 [3, 768, 768], P(None, 'dp', 'tensor')
- qv_bias_grad: float32 [2, 768], P(None, ('dp', 'tensor'))
- out_weight_grad: float32 [768, 768], P('tensor', 'dp')
- out_bias_grad: float32 [768], P(('dp', 'tensor'))
- norm1_gain_grad: float32 [768], P(('dp', 'tensor'))
- norm1_shift_grad: float32 [768], P(('dp', 'tensor'))
- up_weight_grad: float32 [768, 3072], P('dp', 'tensor')
- up_bias_grad: float32 [3072], P(('dp', 'tensor'))
- down_weight_grad: float32 [3072, 768], P('tensor', 'dp')
- down_bias_grad: float32 [768], P(('dp', 'tensor'))
- norm2_gain_grad: float32 [768], P(('dp', 'tensor'))
- norm2_shift_grad: float32 [768], P(('dp', 'tensor'))
Inputs may be any that keep to these rules, and one draw needn't show every extreme that they name: `segment_ids`: in every row of 128 tokens the segment numbers never fall, each number from 0 to 7 occurs on 1 to 32 consecutive tokens, and some sentence has exactly 32 tokens.
All inputs are finite; a program needn't handle non-finite values.
Results may differ from a plain program's by a relative error of at most 0.013.
Values may be sent and summed in bfloat16 or wider, within the bound.
No kernel may reach another device: no remote copies, remote signals or barrier semaphores. Data moves between devices by JAX's collectives and lax.ppermute only.
A program may use at most 128 MiB of HBM per device.

v0:
```python
from functools import partial
import jax
import jax.numpy as jnp
from jax import lax
from jax.sharding import PartitionSpec as P

HD = 64
EPS = 1e-12
NEG = -1000000000.0
highest = lax.Precision.HIGHEST


def round_low(values):
    return lax.optimization_barrier(values.astype(jnp.bfloat16)).astype(jnp.float32)


def normalize(values, gain, shift):
    center = values - jnp.mean(values, axis=-1, keepdims=True)
    inverse = lax.rsqrt(jnp.mean(center * center, axis=-1, keepdims=True) + EPS)
    normed = center * inverse
    return (normed * gain + shift, normed, inverse)


def normalize_back(grad_out, normed, inverse, gain):
    scaled = grad_out * gain
    grad_in = inverse * (
        scaled
        - jnp.mean(scaled, axis=-1, keepdims=True)
        - normed * jnp.mean(scaled * normed, axis=-1, keepdims=True)
    )
    return (grad_in, jnp.sum(grad_out * normed, axis=0), jnp.sum(grad_out, axis=0))


def block_size(seq_count, seq_len):
    largest = max(1, 512 // seq_len)
    chosen = 1
    for trial in range(1, seq_count + 1):
        if seq_count % trial == 0 and trial <= largest:
            chosen = trial
    return chosen


def masked_scores(query_blk, key_blk, seg_blk, score_scale):
    raw_scores = (
        jnp.einsum("gqhd,gkhd->ghqk", query_blk, key_blk, preferred_element_type=jnp.float32)
        * score_scale
    )
    same_segment = seg_blk[:, None, :, None] == seg_blk[:, None, None, :]
    return jnp.where(same_segment, raw_scores, NEG)


def per_device(
    hidden_in,
    segment_ids,
    pooled_grad,
    qkv_weight,
    qv_bias,
    out_weight,
    out_bias,
    norm1_gain,
    norm1_shift,
    up_weight,
    up_bias,
    down_weight,
    down_bias,
    norm2_gain,
    norm2_shift,
):
    micro_total = hidden_in.shape[0]
    rows_local = hidden_in.shape[1]
    model_width = hidden_in.shape[2]
    seq_len = segment_ids.shape[2]
    seqs_local = segment_ids.shape[1]
    seg_count = pooled_grad.shape[2]
    tensor_rank = lax.axis_index("tensor")
    score_scale = float(HD) ** (-0.5)
    gathered = (
        lax.all_gather(qv_bias, ("dp", "tensor"), axis=1, tiled=True),
        lax.all_gather(out_bias, ("dp", "tensor"), axis=0, tiled=True),
        lax.all_gather(norm1_gain, ("dp", "tensor"), axis=0, tiled=True),
        lax.all_gather(norm1_shift, ("dp", "tensor"), axis=0, tiled=True),
        lax.all_gather(up_bias, ("dp", "tensor"), axis=0, tiled=True),
        lax.all_gather(down_bias, ("dp", "tensor"), axis=0, tiled=True),
        lax.all_gather(norm2_gain, ("dp", "tensor"), axis=0, tiled=True),
        lax.all_gather(norm2_shift, ("dp", "tensor"), axis=0, tiled=True),
    )
    qv_full, bias_out, gain_one, shift_one, up_full, bias_down, gain_two, shift_two = tuple(
        (item.astype(jnp.float32) for item in gathered)
    )
    head_cols = qkv_weight.shape[2]
    hidden_cols = up_weight.shape[1]
    heads_local = head_cols // HD
    bias_query = lax.dynamic_slice_in_dim(qv_full[0], tensor_rank * head_cols, head_cols)
    bias_value = lax.dynamic_slice_in_dim(qv_full[1], tensor_rank * head_cols, head_cols)
    bias_up = lax.dynamic_slice_in_dim(up_full, tensor_rank * hidden_cols, hidden_cols)

    def fetch_weights():
        return (
            lax.all_gather(qkv_weight, "dp", axis=1, tiled=True),
            lax.all_gather(out_weight, "dp", axis=1, tiled=True),
            lax.all_gather(up_weight, "dp", axis=0, tiled=True),
            lax.all_gather(down_weight, "dp", axis=1, tiled=True),
        )

    full_shapes = (
        (3, model_width, head_cols),
        (head_cols, model_width),
        (model_width, hidden_cols),
        (hidden_cols, model_width),
    )
    totals = tuple((jnp.zeros(shape_now, jnp.float32) for shape_now in full_shapes))
    qv_grad_local = jnp.zeros((2, head_cols), jnp.float32)
    up_bias_local = jnp.zeros((hidden_cols,), jnp.float32)
    out_bias_part = jnp.zeros((model_width,), jnp.float32)
    down_bias_part = jnp.zeros((model_width,), jnp.float32)
    gain_one_part = jnp.zeros((model_width,), jnp.float32)
    shift_one_part = jnp.zeros((model_width,), jnp.float32)
    gain_two_part = jnp.zeros((model_width,), jnp.float32)
    shift_two_part = jnp.zeros((model_width,), jnp.float32)
    pooled_list = []
    input_list = []
    for batch_index in range(micro_total):
        qkv_now, out_now, up_now, down_now = fetch_weights()
        x_rows = hidden_in[batch_index]
        seg_rows = segment_ids[batch_index]
        x_group, seg_group = (
            lax.all_gather(x_rows, "tensor", axis=0, tiled=True),
            lax.all_gather(seg_rows, "tensor", axis=0, tiled=True),
        )
        tokens_all = x_group.shape[0]
        projected = jnp.einsum("rd,cde->cre", x_group, qkv_now, preferred_element_type=jnp.float32)
        query_rows = (projected[0] + bias_query).astype(jnp.bfloat16)
        key_rows = projected[1].astype(jnp.bfloat16)
        value_rows = (projected[2] + bias_value).astype(jnp.bfloat16)
        seq_group = seg_group.shape[0]
        per_block = block_size(seq_group, seq_len)
        block_total = seq_group // per_block

        def split_heads(tensor_in):
            return tensor_in.reshape(block_total, per_block, seq_len, heads_local, HD)

        seg_blocks = seg_group.reshape(block_total, per_block, seq_len)
        query_blocks = split_heads(query_rows)
        key_blocks = split_heads(key_rows)
        value_blocks = split_heads(value_rows)

        def attend_forward(inputs):
            query_blk, key_blk, value_blk, seg_blk = inputs
            scores = masked_scores(query_blk, key_blk, seg_blk, score_scale)
            row_max = jnp.max(scores, axis=-1, keepdims=True)
            exp_scores = jnp.exp(scores - row_max)
            row_sum = jnp.sum(exp_scores, axis=-1, keepdims=True)
            prob_low = (exp_scores / row_sum).astype(jnp.bfloat16)
            attended_blk = jnp.einsum(
                "ghqk,gkhd->gqhd", prob_low, value_blk, preferred_element_type=jnp.float32
            )
            return (attended_blk.astype(jnp.bfloat16), (row_max + jnp.log(row_sum))[..., 0])

        attended, lse_blocks = lax.map(
            attend_forward, (query_blocks, key_blocks, value_blocks, seg_blocks)
        )
        att_rows = attended.reshape(tokens_all, head_cols)
        branch_one = lax.psum_scatter(
            jnp.dot(att_rows, out_now, preferred_element_type=jnp.float32),
            "tensor",
            scatter_dimension=0,
            tiled=True,
        )
        pre_one = branch_one + bias_out + x_rows.astype(jnp.float32)
        out_one, normed_one, inverse_one = normalize(pre_one, gain_one, shift_one)
        normed_group = lax.all_gather(out_one.astype(jnp.bfloat16), "tensor", axis=0, tiled=True)
        up_act = jnp.dot(normed_group, up_now, preferred_element_type=jnp.float32) + bias_up
        hidden_act = jax.nn.gelu(up_act, approximate=False).astype(jnp.bfloat16)
        branch_two = lax.psum_scatter(
            jnp.dot(hidden_act, down_now, preferred_element_type=jnp.float32),
            "tensor",
            scatter_dimension=0,
            tiled=True,
        )
        pre_two = branch_two + bias_down + out_one
        out_two, normed_two, inverse_two = normalize(pre_two, gain_two, shift_two)
        onehot = (
            seg_rows[:, :, None] == jnp.arange(seg_count, dtype=jnp.int32)[None, None, :]
        ).astype(jnp.float32)
        counts = jnp.sum(onehot, axis=1)
        sums = jnp.einsum(
            "lts,ltd->lsd",
            onehot,
            out_two.reshape(seqs_local, seq_len, model_width),
            precision=highest,
        )
        pooled_list.append(sums / counts[:, :, None])
        grad_out = jnp.einsum(
            "lts,lsd->ltd", onehot, pooled_grad[batch_index] / counts[:, :, None], precision=highest
        ).reshape(rows_local, model_width)
        grad_pre_two, gain_two_now, shift_two_now = normalize_back(
            grad_out, normed_two, inverse_two, gain_two
        )
        gain_two_part = gain_two_part + gain_two_now
        shift_two_part = shift_two_part + shift_two_now
        down_bias_part = down_bias_part + jnp.sum(grad_pre_two, axis=0)
        qkv_back, out_back, up_back, down_back = fetch_weights()
        ffn_grad_group = lax.all_gather(
            grad_pre_two.astype(jnp.bfloat16), "tensor", axis=0, tiled=True
        )
        batch_down = jnp.einsum(
            "rf,rd->fd", hidden_act, ffn_grad_group, preferred_element_type=jnp.float32
        )
        hidden_grad = jnp.einsum(
            "rd,fd->rf", ffn_grad_group, down_back, preferred_element_type=jnp.float32
        )
        gelu_value, gelu_pull = jax.vjp(partial(jax.nn.gelu, approximate=False), up_act)
        up_grad = gelu_pull(hidden_grad)[0].astype(jnp.bfloat16)
        up_bias_local = up_bias_local + jnp.sum(up_grad.astype(jnp.float32), axis=0)
        batch_up = jnp.einsum(
            "rd,rf->df", normed_group, up_grad, preferred_element_type=jnp.float32
        )
        normed_back = lax.psum_scatter(
            jnp.einsum("rf,df->rd", up_grad, up_back, preferred_element_type=jnp.float32),
            "tensor",
            scatter_dimension=0,
            tiled=True,
        )
        normed_grad = round_low(normed_back) + grad_pre_two
        grad_pre_one, gain_one_now, shift_one_now = normalize_back(
            normed_grad, normed_one, inverse_one, gain_one
        )
        gain_one_part = gain_one_part + gain_one_now
        shift_one_part = shift_one_part + shift_one_now
        out_bias_part = out_bias_part + jnp.sum(grad_pre_one, axis=0)
        attn_grad_group = lax.all_gather(
            grad_pre_one.astype(jnp.bfloat16), "tensor", axis=0, tiled=True
        )
        batch_out = jnp.einsum(
            "re,rd->ed", att_rows, attn_grad_group, preferred_element_type=jnp.float32
        )
        att_grad = jnp.einsum(
            "rd,ed->re", attn_grad_group, out_back, preferred_element_type=jnp.float32
        ).astype(jnp.bfloat16)
        att_grad_blocks = split_heads(att_grad)

        def attend_backward(inputs):
            query_blk, key_blk, value_blk, seg_blk, lse_blk, grad_blk = inputs
            scores = masked_scores(query_blk, key_blk, seg_blk, score_scale)
            prob_rows = jnp.exp(scores - lse_blk[..., None])
            value_grad = jnp.einsum(
                "ghqk,gqhd->gkhd",
                prob_rows.astype(jnp.bfloat16),
                grad_blk,
                preferred_element_type=jnp.float32,
            )
            prob_grad = jnp.einsum(
                "gqhd,gkhd->ghqk", grad_blk, value_blk, preferred_element_type=jnp.float32
            )
            score_grad = prob_rows * (
                prob_grad - jnp.sum(prob_rows * prob_grad, axis=-1, keepdims=True)
            )
            score_low = score_grad.astype(jnp.bfloat16)
            query_grad = (
                jnp.einsum(
                    "ghqk,gkhd->gqhd", score_low, key_blk, preferred_element_type=jnp.float32
                )
                * score_scale
            )
            key_grad = (
                jnp.einsum(
                    "ghqk,gqhd->gkhd", score_low, query_blk, preferred_element_type=jnp.float32
                )
                * score_scale
            )
            return (
                query_grad.astype(jnp.bfloat16),
                key_grad.astype(jnp.bfloat16),
                value_grad.astype(jnp.bfloat16),
            )

        query_grads, key_grads, value_grads = lax.map(
            attend_backward,
            (query_blocks, key_blocks, value_blocks, seg_blocks, lse_blocks, att_grad_blocks),
        )
        qkv_grad = jnp.stack(
            [
                query_grads.reshape(tokens_all, head_cols),
                key_grads.reshape(tokens_all, head_cols),
                value_grads.reshape(tokens_all, head_cols),
            ]
        )
        qv_grad_local = qv_grad_local + jnp.stack(
            [
                jnp.sum(qkv_grad[0].astype(jnp.float32), axis=0),
                jnp.sum(qkv_grad[2].astype(jnp.float32), axis=0),
            ]
        )
        batch_qkv = jnp.einsum("rd,cre->cde", x_group, qkv_grad, preferred_element_type=jnp.float32)
        input_back = lax.psum_scatter(
            jnp.einsum(
                "cre,cde->rd", qkv_grad, qkv_back, preferred_element_type=jnp.float32
            ).astype(jnp.bfloat16),
            "tensor",
            scatter_dimension=0,
            tiled=True,
        ).astype(jnp.float32)
        input_list.append(input_back + grad_pre_one)
        totals = tuple(
            (
                running + update
                for running, update in zip(totals, (batch_qkv, batch_out, batch_up, batch_down))
            )
        )
    final_qkv = lax.psum_scatter(totals[0], "dp", scatter_dimension=1, tiled=True)
    final_out = lax.psum_scatter(totals[1], "dp", scatter_dimension=1, tiled=True)
    final_up = lax.psum_scatter(totals[2], "dp", scatter_dimension=0, tiled=True)
    final_down = lax.psum_scatter(totals[3], "dp", scatter_dimension=1, tiled=True)
    qv_place = lax.dynamic_update_slice_in_dim(
        jnp.zeros((2, model_width), jnp.float32), qv_grad_local, tensor_rank * head_cols, 1
    )
    up_place = lax.dynamic_update_slice_in_dim(
        jnp.zeros(up_full.shape, jnp.float32), up_bias_local, tensor_rank * hidden_cols, 0
    )
    vector_out = (
        lax.psum_scatter(qv_place, ("dp", "tensor"), scatter_dimension=1, tiled=True),
        lax.psum_scatter(out_bias_part, ("dp", "tensor"), scatter_dimension=0, tiled=True),
        lax.psum_scatter(gain_one_part, ("dp", "tensor"), scatter_dimension=0, tiled=True),
        lax.psum_scatter(shift_one_part, ("dp", "tensor"), scatter_dimension=0, tiled=True),
        lax.psum_scatter(up_place, ("dp", "tensor"), scatter_dimension=0, tiled=True),
        lax.psum_scatter(down_bias_part, ("dp", "tensor"), scatter_dimension=0, tiled=True),
        lax.psum_scatter(gain_two_part, ("dp", "tensor"), scatter_dimension=0, tiled=True),
        lax.psum_scatter(shift_two_part, ("dp", "tensor"), scatter_dimension=0, tiled=True),
    )
    return (
        jnp.stack(pooled_list),
        jnp.stack(input_list),
        final_qkv,
        vector_out[0],
        final_out,
        vector_out[1],
        vector_out[2],
        vector_out[3],
        final_up,
        vector_out[4],
        final_down,
        vector_out[5],
        vector_out[6],
        vector_out[7],
    )


def solution(mesh):
    return jax.shard_map(
        per_device,
        mesh=mesh,
        in_specs=(
            P(None, ("dp", "tensor"), None),
            P(None, ("dp", "tensor"), None),
            P(None, ("dp", "tensor"), None, None),
            P(None, "dp", "tensor"),
            P(None, ("dp", "tensor")),
            P("tensor", "dp"),
            P(("dp", "tensor")),
            P(("dp", "tensor")),
            P(("dp", "tensor")),
            P("dp", "tensor"),
            P(("dp", "tensor")),
            P("tensor", "dp"),
            P(("dp", "tensor")),
            P(("dp", "tensor")),
            P(("dp", "tensor")),
        ),
        out_specs=(
            P(None, ("dp", "tensor"), None, None),
            P(None, ("dp", "tensor"), None),
            P(None, "dp", "tensor"),
            P(None, ("dp", "tensor")),
            P("tensor", "dp"),
            P(("dp", "tensor")),
            P(("dp", "tensor")),
            P(("dp", "tensor")),
            P("dp", "tensor"),
            P(("dp", "tensor")),
            P("tensor", "dp"),
            P(("dp", "tensor")),
            P(("dp", "tensor")),
            P(("dp", "tensor")),
        ),
        check_vma=False,
    )
```

profile of v0, /device:TPU:0, one launch (start us, length us, event | category | flops | bytes accessed | tf_op | source)
XLA Modules:
  0.0 912.5 jit_solution(8620162350987136270)
XLA Ops:
  10.9 21.3 %all-gather.4 = bf16[1,512,768]{2,1,0:T(8,128)(2,1)S(1)} all-gather(bf16[1,128,768]{2,1,0:T(8,128)(2,1)S(1)} %get-tuple-element.326), channel_id=6, replica_groups=mesh['dp'=8,'tensor'=4] {'tensor'}, dimensions={1}, use_global_device_ids=true | all-gather | bytes 983040 | tf_op jit(solution)/shard_map/all_gather | solution.py:127
  32.2 13.2 %all_gather.101 = bf16[3,768,192]{2,0,1:T(4,128)(2,1)S(1)} all-gather(bf16[3,96,192]{2,0,1:T(4,128)(2,1)S(1)} %copy.216), channel_id=1, replica_groups=mesh['dp'=8,'tensor'=4] {'dp'}, dimensions={1}, use_global_device_ids=true | all-gather | bytes 995328 | tf_op jit(solution)/shard_map/all_gather | solution.py:99
  47.5 9.2 %all-gather.5 = s32[4,1,128]{2,1,0:T(1,128)S(1)} all-gather(s32[1,1,128]{2,1,0:T(1,128)S(1)} %get-tuple-element.363), channel_id=7, replica_groups=mesh['dp'=8,'tensor'=4] {'tensor'}, dimensions={0}, use_global_device_ids=true | all-gather | bytes 2560 | tf_op jit(solution)/shard_map/all_gather | solution.py:128
  56.7 63.3 %all-gather.6 = bf16[32,24,2]{1,2,0:T(2,128)(2,1)S(1)} all-gather(bf16[1,24,2]{1,2,0:T(2,128)(2,1)S(1)} %bitcast.271), channel_id=1, replica_groups=mesh['dp'=8,'tensor'=4] {'dp','tensor'}, dimensions={0}, use_global_device_ids=true | all-gather | bytes 3168 | tf_op jit(solution)/shard_map/all_gather | solution.py:78
  121.5 8.4 all_gather.105
  135.7 27.2 %all-gather.2 = bf16[1,512,768]{2,1,0:T(8,128)(2,1)S(1)} all-gather(bf16[1,128,768]{2,1,0:T(8,128)(2,1)S(1)} %copy-done.79), channel_id=4, replica_groups=mesh['dp'=8,'tensor'=4] {'tensor'}, dimensions={1}, use_global_device_ids=true | all-gather | bytes 983040 | tf_op jit(solution)/shard_map/all_gather | solution.py:127
  166.5 12.2 %all-gather.3 = s32[4,1,128]{2,1,0:T(1,128)S(1)} all-gather(s32[1,1,128]{2,1,0:T(1,128)S(1)} %copy-done.149), channel_id=5, replica_groups=mesh['dp'=8,'tensor'=4] {'tensor'}, dimensions={0}, use_global_device_ids=true | all-gather | bytes 2560 | tf_op jit(solution)/shard_map/all_gather | solution.py:128
  182.2 22.7 %all-gather = bf16[1,512,768]{2,1,0:T(8,128)(2,1)S(1)} all-gather(bf16[1,128,768]{2,1,0:T(8,128)(2,1)S(1)} %get-tuple-element.325), channel_id=2, replica_groups=mesh['dp'=8,'tensor'=4] {'tensor'}, dimensions={1}, use_global_device_ids=true | all-gather | bytes 983040 | tf_op jit(solution)/shard_map/all_gather | solution.py:127
  211.0 11.9 %all-gather.1 = s32[4,1,128]{2,1,0:T(1,128)S(1)} all-gather(s32[1,1,128]{2,1,0:T(1,128)S(1)} %copy-done.148), channel_id=3, replica_groups=mesh['dp'=8,'tensor'=4] {'tensor'}, dimensions={0}, use_global_device_ids=true | all-gather | bytes 2560 | tf_op jit(solution)/shard_map/all_gather | solution.py:128
  229.8 40.1 %all-reduce.16 = (bf16[768]{0:T(1024)(128)(2,1)S(1)}, bf16[768]{0:T(1024)(128)(2,1)S(1)}, bf16[768]{0:T(1024)(128)(2,1)S(1)}, bf16[3072]{0:T(1024)(128)(2,1)S(1)...) all-reduce(bf16[768]{0:T(1024)(128)(2,1)S(1)} %dynamic-update-slice, ...), channel_id=1, replica_groups=mesh['dp'=8,'tensor'=4] {'dp','tensor'}, use_global_device_ids=true, to_apply=%add | all-reduce | flops 7680 | bytes 30720
  275.9 19.0 %all_gather.121 = bf16[512,768]{1,0:T(8,128)(2,1)} all-gather(bf16[128,768]{1,0:T(8,128)(2,1)S(1)} %get-tuple-element.334), channel_id=1, replica_groups=mesh['dp'=8,'tensor'=4] {'tensor'}, dimensions={0}, use_global_device_ids=true | all-gather | bytes 983040 | tf_op jit(solution)/shard_map/all_gather | solution.py:171
  294.9 7.2 multiply_convert_fusion
  305.7 23.8 %all_gather.118 = bf16[512,768]{1,0:T(8,128)(2,1)S(1)} all-gather(bf16[128,768]{1,0:T(8,128)(2,1)} %get-tuple-element.333), channel_id=1, replica_groups=mesh['dp'=8,'tensor'=4] {'tensor'}, dimensions={0}, use_global_device_ids=true | all-gather | bytes 983040 | tf_op jit(solution)/shard_map/all_gather | solution.py:171
  329.5 6.7 multiply_convert_fusion.1
  339.2 21.9 %all_gather.109 = bf16[512,768]{1,0:T(8,128)(2,1)S(1)} all-gather(bf16[128,768]{1,0:T(8,128)(2,1)} %get-tuple-element.332), channel_id=1, replica_groups=mesh['dp'=8,'tensor'=4] {'tensor'}, dimensions={0}, use_global_device_ids=true | all-gather | bytes 983040 | tf_op jit(solution)/shard_map/all_gather | solution.py:171
  361.1 6.9 multiply_convert_fusion.2
  378.5 12.4 %reduce-scatter.28.cloned.1.call-done = f32[128,768]{1,0:T(8,128)} async-done(((f32[512,768]{1,0:T(8,128)}), f32[128,768]{1,0:T(8,128)}) %reduce-scatter.28.cloned.1.call-update) | async-done | bytes 393232 | tf_op jit(solution)/shard_map/reduce_scatter | solution.py:174
  390.9 36.4 %reduce-scatter.24.cloned.1.call-done = f32[128,768]{1,0:T(8,128)} async-done(((f32[512,768]{1,0:T(8,128)}), f32[128,768]{1,0:T(8,128)}) %reduce-scatter.24.cloned.1.call-update) | async-done | bytes 393232 | tf_op jit(solution)/shard_map/reduce_scatter | solution.py:174
  435.1 18.1 %all_gather.126 = bf16[512,768]{1,0:T(8,128)(2,1)S(1)} all-gather(bf16[128,768]{1,0:T(8,128)(2,1)S(1)} %get-tuple-element.357), channel_id=1, replica_groups=mesh['dp'=8,'tensor'=4] {'tensor'}, dimensions={0}, use_global_device_ids=true | all-gather | bytes 983040 | tf_op jit(solution)/shard_map/all_gather | solution.py:203
  458.0 25.1 %all_gather.122 = bf16[512,768]{1,0:T(8,128)(2,1)S(1)} all-gather(bf16[128,768]{1,0:T(8,128)(2,1)} %get-tuple-element.291), channel_id=1, replica_groups=mesh['dp'=8,'tensor'=4] {'tensor'}, dimensions={0}, use_global_device_ids=true | all-gather | bytes 983040 | tf_op jit(solution)/shard_map/all_gather | solution.py:203
  490.4 23.0 %all_gather.124 = bf16[512,768]{1,0:T(8,128)(2,1)S(1)} all-gather(bf16[128,768]{1,0:T(8,128)(2,1)} %get-tuple-element.293), channel_id=1, replica_groups=mesh['dp'=8,'tensor'=4] {'tensor'}, dimensions={0}, use_global_device_ids=true | all-gather | bytes 983040 | tf_op jit(solution)/shard_map/all_gather | solution.py:203
  513.4 4.4 convert_reduce_fusion.1
  525.8 19.4 %reduce-scatter.34.cloned.1.call-done = f32[128,768]{1,0:T(8,128)} async-done(((f32[512,768]{1,0:T(8,128)}), f32[128,768]{1,0:T(8,128)}) %reduce-scatter.34.cloned.1.call-update) | async-done | bytes 393232 | tf_op jit(solution)/shard_map/reduce_scatter | solution.py:218
  549.9 31.9 %reduce-scatter.38.cloned.1.call-done = f32[128,768]{1,0:T(8,128)} async-done(((f32[512,768]{1,0:T(8,128)}), f32[128,768]{1,0:T(8,128)}) %reduce-scatter.38.cloned.1.call-update) | async-done | bytes 393232 | tf_op jit(solution)/shard_map/reduce_scatter | solution.py:218
  585.7 18.7 %all_gather.123 = bf16[512,768]{1,0:T(8,128)(2,1)S(1)} all-gather(bf16[128,768]{1,0:T(8,128)(2,1)S(1)} %convert_element_type.390), channel_id=1, replica_groups=mesh['dp'=8,'tensor'=4] {'tensor'}, dimensions={0}, use_global_device_ids=true | all-gather | bytes 983040 | tf_op jit(solution)/shard_map/all_gather | solution.py:231
  609.2 17.5 %all_gather.125 = bf16[512,768]{1,0:T(8,128)(2,1)S(1)} all-gather(bf16[128,768]{1,0:T(8,128)(2,1)S(1)} %convert_element_type.406), channel_id=1, replica_groups=mesh['dp'=8,'tensor'=4] {'tensor'}, dimensions={0}, use_global_device_ids=true | all-gather | bytes 983040 | tf_op jit(solution)/shard_map/all_gather | solution.py:231
  637.9 17.4 %all_gather.127 = bf16[512,768]{1,0:T(8,128)(2,1)S(1)} all-gather(bf16[128,768]{1,0:T(8,128)(2,1)} %convert_element_type.422), channel_id=1, replica_groups=mesh['dp'=8,'tensor'=4] {'tensor'}, dimensions={0}, use_global_device_ids=true | all-gather | bytes 983040 | tf_op jit(solution)/shard_map/all_gather | solution.py:231
  713.3 41.6 %all-reduce.15 = (f32[2,768]{1,0:T(2,128)S(1)}, f32[768]{0:T(1024)S(1)}, f32[768]{0:T(1024)S(1)}, f32[768]{0:T(1024)S(1)}, f32[3072]{0:T(1024)S(1)}, /*index=5*/...) all-reduce(f32[2,768]{1,0:T(2,128)S(1)} %dynamic_update_slice.38, ...), channel_id=21, replica_groups=mesh['dp'=8,'tensor'=4] {'dp','tensor'}, use_global_device_ids=true, to_apply=%region_55.56.clone | all-reduce | flops 9216 | bytes 73728
  763.3 6.1 reduce-scatter.44.cloned.1.call-done
  771.4 40.9 %reduce-scatter.50.cloned.1.call-done = f32[96,576]{1,0:T(8,128)} async-done(((f32[768,576]{1,0:T(8,128)}), f32[96,576]{1,0:T(8,128)}) %reduce-scatter.50.cloned.1.call-update) | async-done | bytes 221200
  814.2 44.6 %reduce-scatter.48.cloned.1.call-done = f32[768,96]{0,1:T(8,128)} async-done(((f32[768,768]{0,1:T(8,128)}), f32[768,96]{0,1:T(8,128)}) %reduce-scatter.48.cloned.1.call-update) | async-done | bytes 294928 | tf_op jit(solution)/shard_map/reduce_scatter | solution.py:313
  858.8 46.1 %reduce-scatter.46.cloned.1.call-done = f32[96,768]{1,0:T(8,128)} async-done(((f32[768,768]{1,0:T(8,128)}), f32[96,768]{1,0:T(8,128)}) %reduce-scatter.46.cloned.1.call-update) | async-done | bytes 294928 | tf_op jit(solution)/shard_map/reduce_scatter | solution.py:312
  (615 shorter events, 175.5 us)
Async XLA Ops:
  8.0 263.7 %reduce-scatter.30.cloned.1.call-start = ((), (), s32[]{:S(2)}) async-start(), calls=%async_computation.22 | async-start | bytes 1966080 | tf_op jit(solution)/shard_map/reduce_scatter | solution.py:163
  32.2 14.1 %copy-start.27 = (bf16[1,512,768]{2,1,0:T(8,128)(2,1)}, bf16[1,512,768]{2,1,0:T(8,128)(2,1)S(1)}, u32[]{:S(2)}) copy-start(bf16[1,512,768]{2,1,0:T(8,128)(2,1)S(1)} %all-gather.4) | copy-start | bytes 2359300
  45.4 117.5 %copy-start.58 = (bf16[3,768,192]{2,0,1:T(4,128)(2,1)}, bf16[3,768,192]{2,0,1:T(4,128)(2,1)S(1)}, u32[]{:S(2)}) copy-start(bf16[3,768,192]{2,0,1:T(4,128)(2,1)S(1)} %all_gather.101) | copy-start | bytes 2654212
  46.3 74.3 %copy-start.88 = (bf16[192,96]{1,0:T(8,128)(2,1)S(1)}, bf16[192,96]{1,0:T(8,128)(2,1)}, u32[]{:S(2)}) copy-start(bf16[192,96]{1,0:T(8,128)(2,1)} %param.20) | copy-start | bytes 110596
  135.6 136.2 %reduce-scatter.26.cloned.1.call-start = ((), (), s32[]{:S(2)}) async-start(), calls=%async_computation.20 | async-start | bytes 1966080 | tf_op jit(solution)/shard_map/reduce_scatter | solution.py:163
  166.3 14.0 %copy-start.65 = (f32[4,128,3,64]{1,0,3,2:T(4,128)}, f32[4,128,3,64]{1,0,3,2:T(4,128)S(1)}, u32[]{:S(2)}) copy-start(f32[4,128,3,64]{1,0,3,2:T(4,128)S(1)} %squeeze.124) | copy-start | bytes 1179652
  182.1 89.6 %reduce-scatter.22.cloned.1.call-start = ((), (), s32[]{:S(2)}) async-start(), calls=%async_computation.16 | async-start | bytes 1966080 | tf_op jit(solution)/shard_map/reduce_scatter | solution.py:163
  208.6 14.4 %copy-start.53 = (bf16[4,128,3,64]{1,0,3,2:T(4,128)(2,1)}, bf16[4,128,3,64]{1,0,3,2:T(4,128)(2,1)S(1)}, u32[]{:S(2)}) copy-start(bf16[4,128,3,64]{1,0,3,2:T(4,128)(2,1)S(1)} %convert_element_type.351) | copy-start | bytes 589828
  226.7 68.2 %all-gather.10.cloned.1.call-start = ((), (), s32[]{:S(2)}) async-start(), calls=%async_computation.17 | async-start | bytes 1327104 | tf_op jit(solution)/shard_map/all_gather | solution.py:101
  227.3 74.9 %all-gather.12.cloned.1.call-start = ((), (), s32[]{:S(2)}) async-start(), calls=%async_computation.18 | async-start | bytes 1327104 | tf_op jit(solution)/shard_map/all_gather | solution.py:102
  227.8 150.6 %reduce-scatter.32.cloned.1.call-start = ((), (), s32[]{:S(2)}) async-start(), calls=%async_computation.23 | async-start | bytes 1966080 | tf_op jit(solution)/shard_map/reduce_scatter | solution.py:174
  305.6 85.3 %reduce-scatter.28.cloned.1.call-start = ((), (), s32[]{:S(2)}) async-start(), calls=%async_computation.21 | async-start | bytes 1966080 | tf_op jit(solution)/shard_map/reduce_scatter | solution.py:174
  339.1 88.2 %reduce-scatter.24.cloned.1.call-start = ((), (), s32[]{:S(2)}) async-start(), calls=%async_computation.19 | async-start | bytes 1966080 | tf_op jit(solution)/shard_map/reduce_scatter | solution.py:174
  370.8 153.2 %reduce-scatter.42.cloned.1.call-start = ((), (), s32[]{:S(2)}) async-start(), calls=%async_computation.28 | async-start | bytes 1966080 | tf_op jit(solution)/shard_map/reduce_scatter | solution.py:218
  431.8 21.5 %copy-start.169 = (f32[512,768]{1,0:T(8,128)S(1)}, f32[512,768]{1,0:T(8,128)}, u32[]{:S(2)}) copy-start(f32[512,768]{1,0:T(8,128)} %get-tuple-element.373) | copy-start | bytes 4718596
  433.9 19.4 %copy-start.160 = (bf16[768,768]{0,1:T(8,128)(2,1)S(1)}, bf16[768,768]{0,1:T(8,128)(2,1)}, u32[]{:S(2)}) copy-start(bf16[768,768]{0,1:T(8,128)(2,1)} %all-gather.12.cloned.1.call-done) | copy-start | bytes 3538948
  433.9 19.4 %copy-start.168 = (f32[512,768]{1,0:T(8,128)S(1)}, f32[512,768]{1,0:T(8,128)}, u32[]{:S(2)}) copy-start(f32[512,768]{1,0:T(8,128)} %get-tuple-element.312) | copy-start | bytes 4718596
  457.9 87.3 %reduce-scatter.34.cloned.1.call-start = ((), (), s32[]{:S(2)}) async-start(), calls=%async_computation.24 | async-start | bytes 1966080 | tf_op jit(solution)/shard_map/reduce_scatter | solution.py:218
  490.4 91.4 %reduce-scatter.38.cloned.1.call-start = ((), (), s32[]{:S(2)}) async-start(), calls=%async_computation.26 | async-start | bytes 1966080 | tf_op jit(solution)/shard_map/reduce_scatter | solution.py:218
  520.7 239.0 %reduce-scatter.52.cloned.1.call-start = ((), (), s32[]{:S(2)}) async-start(), calls=%async_computation.33 | async-start | bytes 884736
  585.6 21.0 %copy-start.19 = (f32[128,768]{1,0:T(8,128)}, f32[128,768]{1,0:T(8,128)S(1)}, u32[]{:S(2)}) copy-start(f32[128,768]{1,0:T(8,128)S(1)} %get-tuple-element.288) | copy-start | bytes 1179652
  585.6 19.9 %copy-start.48 = (bf16[4,128,3,64]{1,0,3,2:T(4,128)(2,1)S(1)}, bf16[4,128,3,64]{1,0,3,2:T(4,128)(2,1)}, u32[]{:S(2)}) copy-start(bf16[4,128,3,64]{1,0,3,2:T(4,128)(2,1)} %copy-done.47) | copy-start | bytes 589828
  637.9 18.9 %copy-start.45 = (bf16[4,128,3,64]{1,0,3,2:T(4,128)(2,1)S(1)}, bf16[4,128,3,64]{1,0,3,2:T(4,128)(2,1)}, u32[]{:S(2)}) copy-start(bf16[4,128,3,64]{1,0,3,2:T(4,128)(2,1)} %copy-done.44) | copy-start | bytes 589828
  658.3 102.9 %reduce-scatter.40.cloned.1.call-start = ((), (), s32[]{:S(2)}) async-start(), calls=%async_computation.27 | async-start | bytes 983040 | tf_op jit(solution)/shard_map/reduce_scatter | solution.py:295
  673.2 89.1 %reduce-scatter.36.cloned.1.call-start = ((), (), s32[]{:S(2)}) async-start(), calls=%async_computation.25 | async-start | bytes 983040 | tf_op jit(solution)/shard_map/reduce_scatter | solution.py:295
  680.4 89.0 %reduce-scatter.44.cloned.1.call-start = ((), (), s32[]{:S(2)}) async-start(), calls=%async_computation.29 | async-start | bytes 983040 | tf_op jit(solution)/shard_map/reduce_scatter | solution.py:295
  684.5 127.8 %reduce-scatter.50.cloned.1.call-start = ((), (), s32[]{:S(2)}) async-start(), calls=%async_computation.32 | async-start | bytes 2211840
  695.6 163.3 %reduce-scatter.48.cloned.1.call-start = ((), (), s32[]{:S(2)}) async-start(), calls=%async_computation.31 | async-start | bytes 2654208 | tf_op jit(solution)/shard_map/reduce_scatter | solution.py:313
  701.5 203.5 %reduce-scatter.46.cloned.1.call-start = ((), (), s32[]{:S(2)}) async-start(), calls=%async_computation.30 | async-start | bytes 2654208 | tf_op jit(solution)/shard_map/reduce_scatter | solution.py:312
  707.7 53.6 %copy-start.24 = (f32[128,768]{1,0:T(8,128)S(1)}, f32[128,768]{1,0:T(8,128)}, u32[]{:S(2)}) copy-start(f32[128,768]{1,0:T(8,128)} %copy-done.23) | copy-start | bytes 1179652
  708.4 53.9 %copy-start.20 = (f32[128,768]{1,0:T(8,128)S(1)}, f32[128,768]{1,0:T(8,128)}, u32[]{:S(2)}) copy-start(f32[128,768]{1,0:T(8,128)} %copy-done.19) | copy-start | bytes 1179652
  710.5 58.8 %copy-start.22 = (f32[128,768]{1,0:T(8,128)S(1)}, f32[128,768]{1,0:T(8,128)}, u32[]{:S(2)}) copy-start(f32[128,768]{1,0:T(8,128)} %get-tuple-element.356) | copy-start | bytes 1179652
  (156 other events, 522.8 us)
Sparse Core Ops, SparseCore 0:
  135.7 43.5 reduce-scatter.29
  182.2 40.3 reduce-scatter.25
  226.8 34.0 reduce-scatter.21
  305.7 47.1 reduce-scatter.31
  355.1 35.7 reduce-scatter.27
  393.0 34.2 reduce-scatter.23
  458.1 49.3 reduce-scatter.41
  509.7 35.4 reduce-scatter.33
  547.5 34.2 reduce-scatter.37
Sparse Core Ops, SparseCore 1:
  229.0 21.3 all-gather.9
  252.1 23.9 all-gather.11
  658.4 35.3 reduce-scatter.51
  696.1 23.0 reduce-scatter.39
  721.5 23.4 reduce-scatter.35
  747.3 22.0 reduce-scatter.43
  772.6 39.7 reduce-scatter.49
  816.5 42.3 reduce-scatter.47
  862.6 42.3 reduce-scatter.45
where the time goes:
time: 922 us; the launch traced here: 913 us
  blocking collectives  456 us (49%)
  waiting for transfers between devices  239 us (26%)
  matrix products  103 us (11%)
  local copies, waits for them, and re-layouts  58.1 us (6%)
  other arithmetic  37.3 us (4%)
  between operations  18.2 us (2%)
    unnamed x2, blocking collectives  81.7 us
    all_gather x3, blocking collectives, per_device(): lax.all_gather(x_rows, 'tensor', axis=0, tiled=True)  71.3 us
    all_gather x3, blocking collectives, per_device(): lax.all_gather(grad_pre_two.astype(jnp.bfloat16), 'tensor', axis=0, tiled...  66.2 us
    all_gather x3, blocking collectives, per_device(): lax.all_gather(out_one.astype(jnp.bfloat16), 'tensor', axis=0, tiled=True)  64.7 us
    all_gather x1, blocking collectives, per_device(): lax.all_gather(qv_bias, ('dp', 'tensor'), axis=1, tiled=True)  63.3 us
    all_gather x3, blocking collectives, per_device(): lax.all_gather(grad_pre_one.astype(jnp.bfloat16), 'tensor', axis=0, tiled...  53.6 us
    reduce_scatter x3, waiting for transfers between devices, per_device(): lax.psum_scatter(jnp.einsum('rf,df->rd', up_grad, up_back, preferred_elem...  51.3 us
    reduce_scatter x3, waiting for transfers between devices, per_device(): lax.psum_scatter(jnp.dot(hidden_act, down_now, preferred_element_type=jnp...  48.9 us
  transfers between devices with their start and end apart: 18, of which 8 were waited for; matrix products, arithmetic and copies ran while one was open for 15% of the time, Pallas kernels for 0%

commit v1 on v0

--- a/solution.py
+++ b/solution.py
@@ -228,9 +228,25 @@
         gain_one_part = gain_one_part + gain_one_now
         shift_one_part = shift_one_part + shift_one_now
         out_bias_part = out_bias_part + jnp.sum(grad_pre_one, axis=0)
-        attn_grad_group = lax.all_gather(
-            grad_pre_one.astype(jnp.bfloat16), "tensor", axis=0, tiled=True
-        )
+        x = grad_pre_one.astype(jnp.bfloat16)
+        size, position, extent = (lax.axis_size("tensor"), lax.axis_index("tensor"), x.shape[0])
+        forward = [(i, (i + 1) % size) for i in range(size)]
+        behind = [(i, (i - 1) % size) for i in range(size)]
+        out = jnp.zeros((*x.shape[:0], size * extent, *x.shape[0 + 1 :]), x.dtype)
+        out = lax.dynamic_update_slice_in_dim(out, x, position * extent, axis=0)
+        from_left = from_right = x
+        halfway = size // 2
+        for turn in range(1, halfway + 1):
+            from_left = lax.ppermute(from_left, "tensor", forward)
+            out = lax.dynamic_update_slice_in_dim(
+                out, from_left, (position - turn) % size * extent, axis=0
+            )
+            if turn < size - halfway:
+                from_right = lax.ppermute(from_right, "tensor", behind)
+                out = lax.dynamic_update_slice_in_dim(
+                    out, from_right, (position + turn) % size * extent, axis=0
+                )
+        attn_grad_group = out
         batch_out = jnp.einsum(
             "re,rd->ed", att_rows, attn_grad_group, preferred_element_type=jnp.float32
         )

time: 922 us -> 896 us (0.972)
  blocking collectives: 456 us -> 392 us
  starting transfers between devices: 1.11 us -> 18.6 us
  local copies, waits for them, and re-layouts: 58.1 us -> 75.3 us
    all_gather x3 -> x0, blocking collectives: 53.6 us -> none  [per_device(): lax.all_gather(grad_pre_one.astype(jnp.bfloat16), 'tensor', axis=0, tiled...]
    ppermute x0 -> x9, starting transfers between devices: none -> 17.1 us  [the longest x3 10.7 us: per_device(): from_right = lax.ppermute(from_right, 'tensor', behind)]
    ppermute x0 -> x9, waiting for transfers between devices: none -> 14.8 us  [the longest x6 14.8 us: per_device(): from_left = lax.ppermute(from_left, 'tensor', forward)]
    unnamed x376 -> x386, local copies, waits for them, and re-layouts: 39 us -> 44.4 us
  transfers between devices with their start and end apart: 18 -> 27, of which waited for: 8 -> 12; matrix products, arithmetic and copies ran while one was open for 15% -> 18% of each run, Pallas kernels for 0% -> 0%
where the time goes in v1:
time: 896 us; the launch traced here: 886 us
  blocking collectives  392 us (44%)
  waiting for transfers between devices  242 us (27%)
  matrix products  98.5 us (11%)
  local copies, waits for them, and re-layouts  75.3 us (8%)
  other arithmetic  40.3 us (4%)
  starting transfers between devices  18.6 us (2%)
  between operations  18.5 us (2%)
    unnamed x2, blocking collectives  80.9 us
    all_gather x3, blocking collectives, per_device(): lax.all_gather(grad_pre_two.astype(jnp.bfloat16), 'tensor', axis=0, tiled...  66.7 us
    all_gather x1, blocking collectives, per_device(): lax.all_gather(qv_bias, ('dp', 'tensor'), axis=1, tiled=True)  65.5 us
    all_gather x3, blocking collectives, per_device(): lax.all_gather(out_one.astype(jnp.bfloat16), 'tensor', axis=0, tiled=True)  65 us
    all_gather x3, blocking collectives, per_device(): lax.all_gather(x_rows, 'tensor', axis=0, tiled=True)  64 us
    reduce_scatter x3, waiting for transfers between devices, per_device(): lax.psum_scatter(jnp.dot(hidden_act, down_now, preferred_element_type=jnp...  48.6 us
    reduce_scatter x1, waiting for transfers between devices, per_device(): lax.psum_scatter(totals[3], 'dp', scatter_dimension=1, tiled=True)  46.1 us
    reduce_scatter x3, waiting for transfers between devices, per_device(): lax.psum_scatter(jnp.einsum('rf,df->rd', up_grad, up_back, preferred_elem...  45.1 us
  transfers between devices with their start and end apart: 27, of which 12 were waited for; matrix products, arithmetic and copies ran while one was open for 18% of the time, Pallas kernels for 0%

profile of v1, /device:TPU:0, one launch (start us, length us, event | category | flops | bytes accessed | tf_op | source)
XLA Modules:
  0.0 885.9 jit_solution(8292244380391928972)
XLA Ops:
  10.0 21.3 %all-gather = bf16[1,512,768]{2,1,0:T(8,128)(2,1)S(1)} all-gather(bf16[1,128,768]{2,1,0:T(8,128)(2,1)S(1)} %get-tuple-element.331), channel_id=2, replica_groups=mesh['dp'=8,'tensor'=4] {'tensor'}, dimensions={1}, use_global_device_ids=true | all-gather | bytes 983040 | tf_op jit(solution)/shard_map/all_gather | solution.py:127
  31.4 13.2 %all_gather.92 = bf16[3,768,192]{2,0,1:T(4,128)(2,1)S(1)} all-gather(bf16[3,96,192]{2,0,1:T(4,128)(2,1)S(1)} %copy.216), channel_id=1, replica_groups=mesh['dp'=8,'tensor'=4] {'dp'}, dimensions={1}, use_global_device_ids=true | all-gather | bytes 995328 | tf_op jit(solution)/shard_map/all_gather | solution.py:99
  46.4 8.4 all_gather.96
  55.1 65.5 %all-gather.6 = bf16[32,24,2]{1,2,0:T(2,128)(2,1)S(1)} all-gather(bf16[1,24,2]{1,2,0:T(2,128)(2,1)S(1)} %bitcast.271), channel_id=1, replica_groups=mesh['dp'=8,'tensor'=4] {'dp','tensor'}, dimensions={0}, use_global_device_ids=true | all-gather | bytes 3168 | tf_op jit(solution)/shard_map/all_gather | solution.py:78
  122.3 7.5 all-gather.1
  134.4 23.2 %all-gather.2 = bf16[1,512,768]{2,1,0:T(8,128)(2,1)S(1)} all-gather(bf16[1,128,768]{2,1,0:T(8,128)(2,1)} %get-tuple-element.333), channel_id=4, replica_groups=mesh['dp'=8,'tensor'=4] {'tensor'}, dimensions={1}, use_global_device_ids=true | all-gather | bytes 983040 | tf_op jit(solution)/shard_map/all_gather | solution.py:127
  161.3 11.8 %all-gather.3 = s32[4,1,128]{2,1,0:T(1,128)S(1)} all-gather(s32[1,1,128]{2,1,0:T(1,128)S(1)} %copy-done.152), channel_id=5, replica_groups=mesh['dp'=8,'tensor'=4] {'tensor'}, dimensions={0}, use_global_device_ids=true | all-gather | bytes 2560 | tf_op jit(solution)/shard_map/all_gather | solution.py:128
  176.9 19.5 %all-gather.4 = bf16[1,512,768]{2,1,0:T(8,128)(2,1)S(1)} all-gather(bf16[1,128,768]{2,1,0:T(8,128)(2,1)} %get-tuple-element.332), channel_id=6, replica_groups=mesh['dp'=8,'tensor'=4] {'tensor'}, dimensions={1}, use_global_device_ids=true | all-gather | bytes 983040 | tf_op jit(solution)/shard_map/all_gather | solution.py:127
  200.7 9.3 %all-gather.5 = s32[4,1,128]{2,1,0:T(1,128)S(1)} all-gather(s32[1,1,128]{2,1,0:T(1,128)S(1)} %copy-done.151), channel_id=7, replica_groups=mesh['dp'=8,'tensor'=4] {'tensor'}, dimensions={0}, use_global_device_ids=true | all-gather | bytes 2560 | tf_op jit(solution)/shard_map/all_gather | solution.py:128
  216.9 41.4 %all-reduce.16 = (bf16[768]{0:T(1024)(128)(2,1)S(1)}, bf16[768]{0:T(1024)(128)(2,1)S(1)}, bf16[768]{0:T(1024)(128)(2,1)S(1)}, bf16[3072]{0:T(1024)(128)(2,1)S(1)...) all-reduce(bf16[768]{0:T(1024)(128)(2,1)S(1)} %dynamic-update-slice, ...), channel_id=1, replica_groups=mesh['dp'=8,'tensor'=4] {'dp','tensor'}, use_global_device_ids=true, to_apply=%add | all-reduce | flops 7680 | bytes 30720
  264.3 18.8 %all_gather.100 = bf16[512,768]{1,0:T(8,128)(2,1)} all-gather(bf16[128,768]{1,0:T(8,128)(2,1)S(1)} %get-tuple-element.338), channel_id=1, replica_groups=mesh['dp'=8,'tensor'=4] {'tensor'}, dimensions={0}, use_global_device_ids=true | all-gather | bytes 983040 | tf_op jit(solution)/shard_map/all_gather | solution.py:171
  283.1 7.2 multiply_convert_fusion.2
  293.9 24.5 %all_gather.109 = bf16[512,768]{1,0:T(8,128)(2,1)S(1)} all-gather(bf16[128,768]{1,0:T(8,128)(2,1)} %get-tuple-element.339), channel_id=1, replica_groups=mesh['dp'=8,'tensor'=4] {'tensor'}, dimensions={0}, use_global_device_ids=true | all-gather | bytes 983040 | tf_op jit(solution)/shard_map/all_gather | solution.py:171
  318.4 6.8 multiply_convert_fusion.1
  328.1 21.7 %all_gather.112 = bf16[512,768]{1,0:T(8,128)(2,1)S(1)} all-gather(bf16[128,768]{1,0:T(8,128)(2,1)} %get-tuple-element.340), channel_id=1, replica_groups=mesh['dp'=8,'tensor'=4] {'tensor'}, dimensions={0}, use_global_device_ids=true | all-gather | bytes 983040 | tf_op jit(solution)/shard_map/all_gather | solution.py:171
  349.8 6.7 multiply_convert_fusion
  367.1 12.1 %reduce-scatter.28.cloned.1.call-done = f32[128,768]{1,0:T(8,128)} async-done(((f32[512,768]{1,0:T(8,128)}), f32[128,768]{1,0:T(8,128)}) %reduce-scatter.28.cloned.1.call-update) | async-done | bytes 393232 | tf_op jit(solution)/shard_map/reduce_scatter | solution.py:174
  379.2 36.4 %reduce-scatter.32.cloned.1.call-done = f32[128,768]{1,0:T(8,128)} async-done(((f32[512,768]{1,0:T(8,128)}), f32[128,768]{1,0:T(8,128)}) %reduce-scatter.32.cloned.1.call-update) | async-done | bytes 393232 | tf_op jit(solution)/shard_map/reduce_scatter | solution.py:174
  422.4 18.2 %all_gather.113 = bf16[512,768]{1,0:T(8,128)(2,1)S(1)} all-gather(bf16[128,768]{1,0:T(8,128)(2,1)S(1)} %get-tuple-element.293), channel_id=1, replica_groups=mesh['dp'=8,'tensor'=4] {'tensor'}, dimensions={0}, use_global_device_ids=true | all-gather | bytes 983040 | tf_op jit(solution)/shard_map/all_gather | solution.py:203
  450.6 28.3 %all_gather.115 = bf16[512,768]{1,0:T(8,128)(2,1)S(1)} all-gather(bf16[128,768]{1,0:T(8,128)(2,1)S(1)} %get-tuple-element.363), channel_id=1, replica_groups=mesh['dp'=8,'tensor'=4] {'tensor'}, dimensions={0}, use_global_device_ids=true | all-gather | bytes 983040 | tf_op jit(solution)/shard_map/all_gather | solution.py:203
  485.5 20.2 %all_gather.114 = bf16[512,768]{1,0:T(8,128)(2,1)S(1)} all-gather(bf16[128,768]{1,0:T(8,128)(2,1)} %get-tuple-element.297), channel_id=1, replica_groups=mesh['dp'=8,'tensor'=4] {'tensor'}, dimensions={0}, use_global_device_ids=true | all-gather | bytes 983040 | tf_op jit(solution)/shard_map/all_gather | solution.py:203
  505.7 4.3 convert_reduce_fusion.1
  518.5 12.6 %reduce-scatter.42.cloned.1.call-done = f32[128,768]{1,0:T(8,128)} async-done(((f32[512,768]{1,0:T(8,128)}), f32[128,768]{1,0:T(8,128)}) %reduce-scatter.42.cloned.1.call-update) | async-done | bytes 393232 | tf_op jit(solution)/shard_map/reduce_scatter | solution.py:218
  535.9 32.5 %reduce-scatter.38.cloned.1.call-done = f32[128,768]{1,0:T(8,128)} async-done(((f32[512,768]{1,0:T(8,128)}), f32[128,768]{1,0:T(8,128)}) %reduce-scatter.38.cloned.1.call-update) | async-done | bytes 393232 | tf_op jit(solution)/shard_map/reduce_scatter | solution.py:218
  586.6 5.1 collective-permute-done.3
  594.2 6.0 collective-permute-done
  667.4 4.2 copy.281
  671.7 4.7 reshape.805
  693.8 39.5 %all-reduce.15 = (f32[2,768]{1,0:T(2,128)S(1)}, f32[768]{0:T(1024)S(1)}, f32[768]{0:T(1024)S(1)}, f32[768]{0:T(1024)S(1)}, f32[3072]{0:T(1024)S(1)}, /*index=5*/...) all-reduce(f32[2,768]{1,0:T(2,128)S(1)} %dynamic_update_slice.86, ...), channel_id=21, replica_groups=mesh['dp'=8,'tensor'=4] {'dp','tensor'}, use_global_device_ids=true, to_apply=%region_55.56.clone | all-reduce | flops 9216 | bytes 73728
  744.8 40.9 %reduce-scatter.50.cloned.1.call-done = f32[96,576]{1,0:T(8,128)} async-done(((f32[768,576]{1,0:T(8,128)}), f32[96,576]{1,0:T(8,128)}) %reduce-scatter.50.cloned.1.call-update) | async-done | bytes 221200
  787.6 44.6 %reduce-scatter.46.cloned.1.call-done = f32[96,768]{1,0:T(8,128)} async-done(((f32[768,768]{1,0:T(8,128)}), f32[96,768]{1,0:T(8,128)}) %reduce-scatter.46.cloned.1.call-update) | async-done | bytes 294928 | tf_op jit(solution)/shard_map/reduce_scatter | solution.py:328
  832.2 46.1 %reduce-scatter.48.cloned.1.call-done = f32[768,96]{0,1:T(8,128)} async-done(((f32[768,768]{0,1:T(8,128)}), f32[768,96]{0,1:T(8,128)}) %reduce-scatter.48.cloned.1.call-update) | async-done | bytes 294928 | tf_op jit(solution)/shard_map/reduce_scatter | solution.py:329
  (652 shorter events, 204.9 us)
Async XLA Ops:
  8.0 252.1 %reduce-scatter.22.cloned.1.call-start = ((), (), s32[]{:S(2)}) async-start(), calls=%async_computation.16 | async-start | bytes 1966080 | tf_op jit(solution)/shard_map/reduce_scatter | solution.py:163
  44.6 113.1 %copy-start.63 = (bf16[3,768,192]{2,0,1:T(4,128)(2,1)}, bf16[3,768,192]{2,0,1:T(4,128)(2,1)S(1)}, u32[]{:S(2)}) copy-start(bf16[3,768,192]{2,0,1:T(4,128)(2,1)S(1)} %all_gather.92) | copy-start | bytes 2654212
  54.9 76.5 %copy-start.54 = (bf16[4,128,3,64]{1,0,3,2:T(4,128)(2,1)}, bf16[4,128,3,64]{1,0,3,2:T(4,128)(2,1)S(1)}, u32[]{:S(2)}) copy-start(bf16[4,128,3,64]{1,0,3,2:T(4,128)(2,1)S(1)} %convert_element_type.351) | copy-start | bytes 589828
  55.1 76.5 %copy-start.15 = (f32[4,128,3,64]{1,0,3,2:T(4,128)}, f32[4,128,3,64]{1,0,3,2:T(4,128)S(1)}, u32[]{:S(2)}) copy-start(f32[4,128,3,64]{1,0,3,2:T(4,128)S(1)} %squeeze.122) | copy-start | bytes 1179652
  134.4 125.8 %reduce-scatter.26.cloned.1.call-start = ((), (), s32[]{:S(2)}) async-start(), calls=%async_computation.20 | async-start | bytes 1966080 | tf_op jit(solution)/shard_map/reduce_scatter | solution.py:163
  176.9 83.3 %reduce-scatter.30.cloned.1.call-start = ((), (), s32[]{:S(2)}) async-start(), calls=%async_computation.22 | async-start | bytes 1966080 | tf_op jit(solution)/shard_map/reduce_scatter | solution.py:163
  213.8 69.3 %all-gather.10.cloned.1.call-start = ((), (), s32[]{:S(2)}) async-start(), calls=%async_computation.17 | async-start | bytes 1327104 | tf_op jit(solution)/shard_map/all_gather | solution.py:101
  214.4 75.9 %all-gather.12.cloned.1.call-start = ((), (), s32[]{:S(2)}) async-start(), calls=%async_computation.18 | async-start | bytes 1327104 | tf_op jit(solution)/shard_map/all_gather | solution.py:102
  215.0 152.1 %reduce-scatter.24.cloned.1.call-start = ((), (), s32[]{:S(2)}) async-start(), calls=%async_computation.19 | async-start | bytes 1966080 | tf_op jit(solution)/shard_map/reduce_scatter | solution.py:174
  293.9 85.3 %reduce-scatter.28.cloned.1.call-start = ((), (), s32[]{:S(2)}) async-start(), calls=%async_computation.21 | async-start | bytes 1966080 | tf_op jit(solution)/shard_map/reduce_scatter | solution.py:174
  328.0 87.6 %reduce-scatter.32.cloned.1.call-start = ((), (), s32[]{:S(2)}) async-start(), calls=%async_computation.23 | async-start | bytes 1966080 | tf_op jit(solution)/shard_map/reduce_scatter | solution.py:174
  359.4 157.4 %reduce-scatter.34.cloned.1.call-start = ((), (), s32[]{:S(2)}) async-start(), calls=%async_computation.24 | async-start | bytes 1966080 | tf_op jit(solution)/shard_map/reduce_scatter | solution.py:218
  445.3 85.8 %reduce-scatter.42.cloned.1.call-start = ((), (), s32[]{:S(2)}) async-start(), calls=%async_computation.28 | async-start | bytes 1966080 | tf_op jit(solution)/shard_map/reduce_scatter | solution.py:218
  485.4 82.9 %reduce-scatter.38.cloned.1.call-start = ((), (), s32[]{:S(2)}) async-start(), calls=%async_computation.26 | async-start | bytes 1966080 | tf_op jit(solution)/shard_map/reduce_scatter | solution.py:218
  512.9 225.2 %reduce-scatter.52.cloned.1.call-start = ((), (), s32[]{:S(2)}) async-start(), calls=%async_computation.33 | async-start | bytes 884736
  573.4 9.7 %collective-permute-start.6 = (bf16[128,768]{1,0:T(8,128)(2,1)S(1)}, bf16[128,768]{1,0:T(8,128)(2,1)S(1)}, u32[]{:S(2)}, u32[]{:S(2)}) collective-permute-start(bf16[128,768]{1,0:T(8,128)(2,1)S(1)} %get-tuple-element.300), channel_id=1, source_target_pairs={{0,1},{1,2},{2,3},{3,0},{4,5},{5,6},{6,7},{7,4},{8,9},{9,10},{10,1... | collective-permute-start | bytes 589832 | tf_op jit(solution)/shard_map/ppermute | solution.py:240
  573.9 28.7 %collective-permute-start.7 = (bf16[128,768]{1,0:T(8,128)(2,1)S(1)}, bf16[128,768]{1,0:T(8,128)(2,1)S(1)}, u32[]{:S(2)}, u32[]{:S(2)}) collective-permute-start(bf16[128,768]{1,0:T(8,128)(2,1)S(1)} %get-tuple-element.300), channel_id=1, source_target_pairs={{0,3},{1,0},{2,1},{3,2},{4,7},{5,4},{6,5},{7,6},{8,11},{9,8},{10,9... | collective-permute-start | bytes 589832 | tf_op jit(solution)/shard_map/ppermute | solution.py:245
  577.4 14.2 %collective-permute-start.3 = (bf16[128,768]{1,0:T(8,128)(2,1)S(1)}, bf16[128,768]{1,0:T(8,128)(2,1)}, u32[]{:S(2)}, u32[]{:S(2)}) collective-permute-start(bf16[128,768]{1,0:T(8,128)(2,1)S(1)} %get-tuple-element.296), channel_id=1, source_target_pairs={{0,1},{1,2},{2,3},{3,0},{4,5},{5,6},{6,7},{7,4},{8,9},{9,10},{10,1... | collective-permute-start | bytes 589832 | tf_op jit(solution)/shard_map/ppermute | solution.py:240
  577.5 27.9 %collective-permute-start.4 = (bf16[128,768]{1,0:T(8,128)(2,1)S(1)}, bf16[128,768]{1,0:T(8,128)(2,1)S(1)}, u32[]{:S(2)}, u32[]{:S(2)}) collective-permute-start(bf16[128,768]{1,0:T(8,128)(2,1)S(1)} %get-tuple-element.296), channel_id=1, source_target_pairs={{0,3},{1,0},{2,1},{3,2},{4,7},{5,4},{6,5},{7,6},{8,11},{9,8},{10,9... | collective-permute-start | bytes 589832 | tf_op jit(solution)/shard_map/ppermute | solution.py:245
  581.4 18.7 %collective-permute-start = (bf16[128,768]{1,0:T(8,128)(2,1)S(1)}, bf16[128,768]{1,0:T(8,128)(2,1)}, u32[]{:S(2)}, u32[]{:S(2)}) collective-permute-start(bf16[128,768]{1,0:T(8,128)(2,1)S(1)} %get-tuple-element.292), channel_id=1, source_target_pairs={{0,1},{1,2},{2,3},{3,0},{4,5},{5,6},{6,7},{7,4},{8,9},{9,10},{10,1... | collective-permute-start | bytes 589832 | tf_op jit(solution)/shard_map/ppermute | solution.py:240
  583.1 22.4 %collective-permute-start.1 = (bf16[128,768]{1,0:T(8,128)(2,1)S(1)}, bf16[128,768]{1,0:T(8,128)(2,1)S(1)}, u32[]{:S(2)}, u32[]{:S(2)}) collective-permute-start(bf16[128,768]{1,0:T(8,128)(2,1)S(1)} %get-tuple-element.292), channel_id=1, source_target_pairs={{0,3},{1,0},{2,1},{3,2},{4,7},{5,4},{6,5},{7,6},{8,11},{9,8},{10,9... | collective-permute-start | bytes 589832 | tf_op jit(solution)/shard_map/ppermute | solution.py:245
  591.7 16.8 %collective-permute-start.8 = (bf16[128,768]{1,0:T(8,128)(2,1)S(1)}, bf16[128,768]{1,0:T(8,128)(2,1)S(1)}, u32[]{:S(2)}, u32[]{:S(2)}) collective-permute-start(bf16[128,768]{1,0:T(8,128)(2,1)S(1)} %collective-permute-done.6), channel_id=1, source_target_pairs={{0,1},{1,2},{2,3},{3,0},{4,5},{5,6},{6,7},{7,4},{8,9},{9,10},{10,1... | collective-permute-start | bytes 589832 | tf_op jit(solution)/shard_map/ppermute | solution.py:240
  600.1 28.1 %collective-permute-start.5 = (bf16[128,768]{1,0:T(8,128)(2,1)}, bf16[128,768]{1,0:T(8,128)(2,1)}, u32[]{:S(2)}, u32[]{:S(2)}) collective-permute-start(bf16[128,768]{1,0:T(8,128)(2,1)} %collective-permute-done.3), channel_id=1, source_target_pairs={{0,1},{1,2},{2,3},{3,0},{4,5},{5,6},{6,7},{7,4},{8,9},{9,10},{10,1... | collective-permute-start | bytes 589832 | tf_op jit(solution)/shard_map/ppermute | solution.py:240
  602.6 27.0 %collective-permute-start.2 = (bf16[128,768]{1,0:T(8,128)(2,1)}, bf16[128,768]{1,0:T(8,128)(2,1)}, u32[]{:S(2)}, u32[]{:S(2)}) collective-permute-start(bf16[128,768]{1,0:T(8,128)(2,1)} %collective-permute-done), channel_id=1, source_target_pairs={{0,1},{1,2},{2,3},{3,0},{4,5},{5,6},{6,7},{7,4},{8,9},{9,10},{10,1... | collective-permute-start | bytes 589832 | tf_op jit(solution)/shard_map/ppermute | solution.py:240
  634.1 105.6 %reduce-scatter.44.cloned.1.call-start = ((), (), s32[]{:S(2)}) async-start(), calls=%async_computation.29 | async-start | bytes 983040 | tf_op jit(solution)/shard_map/reduce_scatter | solution.py:311
  643.4 97.3 %reduce-scatter.40.cloned.1.call-start = ((), (), s32[]{:S(2)}) async-start(), calls=%async_computation.27 | async-start | bytes 983040 | tf_op jit(solution)/shard_map/reduce_scatter | solution.py:311
  656.1 86.7 %reduce-scatter.36.cloned.1.call-start = ((), (), s32[]{:S(2)}) async-start(), calls=%async_computation.25 | async-start | bytes 983040 | tf_op jit(solution)/shard_map/reduce_scatter | solution.py:311
  662.3 123.4 %reduce-scatter.50.cloned.1.call-start = ((), (), s32[]{:S(2)}) async-start(), calls=%async_computation.32 | async-start | bytes 2211840
  676.4 155.8 %reduce-scatter.46.cloned.1.call-start = ((), (), s32[]{:S(2)}) async-start(), calls=%async_computation.30 | async-start | bytes 2654208 | tf_op jit(solution)/shard_map/reduce_scatter | solution.py:328
  682.3 196.0 %reduce-scatter.48.cloned.1.call-start = ((), (), s32[]{:S(2)}) async-start(), calls=%async_computation.31 | async-start | bytes 2654208 | tf_op jit(solution)/shard_map/reduce_scatter | solution.py:329
  689.2 51.5 %copy-start.27 = (f32[128,768]{1,0:T(8,128)S(1)}, f32[128,768]{1,0:T(8,128)}, u32[]{:S(2)}) copy-start(f32[128,768]{1,0:T(8,128)} %copy-done.26) | copy-start | bytes 1179652
  690.8 52.0 %copy-start.25 = (f32[128,768]{1,0:T(8,128)S(1)}, f32[128,768]{1,0:T(8,128)}, u32[]{:S(2)}) copy-start(f32[128,768]{1,0:T(8,128)} %copy-done.24) | copy-start | bytes 1179652
  (170 other events, 761.0 us)
Sparse Core Ops, SparseCore 0:
  134.5 43.2 reduce-scatter.21
  180.1 38.0 reduce-scatter.25
  220.5 34.6 reduce-scatter.29
  294.0 47.1 reduce-scatter.23
  343.4 35.7 reduce-scatter.27
  381.3 34.2 reduce-scatter.31
  445.5 46.5 reduce-scatter.33
  494.4 36.7 reduce-scatter.41
  533.4 34.8 reduce-scatter.37
Sparse Core Ops, SparseCore 1:
  216.2 21.4 all-gather.9
  239.4 24.0 all-gather.11
  634.2 33.1 reduce-scatter.51
  669.7 23.0 reduce-scatter.43
  695.0 23.2 reduce-scatter.39
  720.6 22.1 reduce-scatter.35
  746.0 39.6 reduce-scatter.49
  789.9 42.3 reduce-scatter.45
  836.0 42.3 reduce-scatter.47
